TPU v7x, 128 devices: a whole 4x4x4 slice. The times are simulated.
128 devices in a mesh: dx: 8 (over y_lo, x), dy: 16 (over y_hi, z, core).
Axes of the slice: x: 4, y: 4 (y_hi: 2, y_lo: 2; y = y_hi * 2 + y_lo), z: 4, core: 2. Of those that a mesh axis runs over, the one named last changes fastest.
Arguments:
- fine_nodes: bfloat16 [256, 256, 512], P('dx', 'dy'), may hold values from -6 to 6
- fine_edges: bfloat16 [6, 256, 256, 512], P(None, 'dx', 'dy'), may hold values from -6 to 6
- fine_links: int32 [6, 256, 256], P(None, 'dx', 'dy'), may hold values from 0 to 48
- mid_nodes: bfloat16 [64, 64, 512], P('dx', 'dy'), may hold values from -6 to 6
- mid_edges: bfloat16 [6, 64, 64, 512], P(None, 'dx', 'dy'), may hold values from -6 to 6
- mid_links: int32 [6, 64, 64], P(None, 'dx', 'dy'), may hold values from 0 to 8
- coarse_nodes: bfloat16 [16, 16, 512], replicated, may hold values from -6 to 6
- coarse_edges: bfloat16 [6, 16, 16, 512], replicated, may hold values from -6 to 6
- coarse_links: int32 [6, 16, 16], replicated, may hold values from 0 to 255
- edge_self: bfloat16 [1, 512, 1536], replicated, may hold values from -0.25 to 0.25
- edge_sender: bfloat16 [1, 512, 1536], replicated, may hold values from -0.25 to 0.25
- edge_receiver: bfloat16 [1, 512, 1536], replicated, may hold values from -0.25 to 0.25
- edge_bias: float32 [1, 1536], replicated, may hold values from -6 to 6
- edge_output: bfloat16 [1, 1536, 512], replicated, may hold values from -0.15625 to 0.15625
- edge_gain: float32 [1, 512], replicated, may hold values from 0.1 to 1.9
- edge_shift: float32 [1, 512], replicated, may hold values from -3 to 3
- node_self: bfloat16 [1, 512, 1536], replicated, may hold values from -0.25 to 0.25
- node_summed: bfloat16 [1, 512, 1536], replicated, may hold values from -0.109375 to 0.109375
- node_bias: float32 [1, 1536], replicated, may hold values from -6 to 6
- node_output: bfloat16 [1, 1536, 512], replicated, may hold values from -0.15625 to 0.15625
- node_gain: float32 [1, 512], replicated, may hold values from 0.1 to 1.9
- node_shift: float32 [1, 512], replicated, may hold values from -3 to 3
- prolongation: bfloat16 [1, 512, 512], replicated, may hold values from -0.25 to 0.25
- pooling: bfloat16 [1, 512, 512], replicated, may hold values from -0.25 to 0.25
Outputs:
- fine_out: bfloat16 [256, 256, 512], P('dx', 'dy')
- fine_edges_out: bfloat16 [6, 256, 256, 512], P(None, 'dx', 'dy')
- mid_out: bfloat16 [64, 64, 512], P('dx', 'dy')
- mid_edges_out: bfloat16 [6, 64, 64, 512], P(None, 'dx', 'dy')
- coarse_out: bfloat16 [16, 16, 512], replicated
- coarse_edges_out: bfloat16 [6, 16, 16, 512], replicated
Inputs may be any that keep to these rules, and one draw needn't show every extreme that they name: `fine_links`: code q names the sender at offset (q // 7 - 3, q % 7 - 3) from the receiver. `mid_links`: code q names the sender at offset (q // 3 - 1, q % 3 - 1) from the receiver.
All inputs are finite; a program needn't handle non-finite values.
Results may differ from a plain program's by a relative error of at most 0.012.
Values may be sent and summed in bfloat16 or wider, within the bound.
No kernel may reach another device: no remote copies, remote signals or barrier semaphores. Data moves between devices by JAX's collectives and lax.ppermute only.
A program may use at most 128 MiB of HBM per device.

v0:
```python
import jax
import jax.numpy as jnp
from jax import lax
from jax.sharding import Mesh
from jax.sharding import PartitionSpec as P

FINE_REACH = 3
MID_REACH = 1
DX = ("dx_0", "dx_1")
DY = ("dy_0", "dy_1", "dy_2")


epsilon = 1e-05


def with_halo(value, sides, width):
    for axis, dim in sides:
        count, length = (lax.axis_size(axis), value.shape[dim])
        up = [(i, (i + 1) % count) for i in range(count)]
        down = [(j, i) for i, j in up]
        last = lax.slice_in_dim(value, length - width, length, axis=dim)
        leading = lax.slice_in_dim(value, 0, width, axis=dim)
        before = lax.ppermute(last, axis, up)
        after = lax.ppermute(leading, axis, down)
        value = jnp.concatenate([before, value, after], axis=dim)
    return value


def joined_along(blocks, dim):
    dims = list(blocks.shape[1:])
    dims[dim] *= blocks.shape[0]
    return jnp.moveaxis(blocks, 0, dim).reshape(dims)


def all_blocks(value, axes, turns):
    blocks = value[None]
    for k in turns:
        blocks = lax.all_gather(blocks, axes[k], axis=0, tiled=True)
    block = [lax.axis_size(axes[k]) for k in reversed(turns)]
    blocks = blocks.reshape(*block, *value.shape)
    turned = sorted(range(len(turns)), key=lambda place: turns[len(turns) - 1 - place])
    return blocks.transpose(*turned, *range(len(turns), blocks.ndim)).reshape(-1, *value.shape)


def gather_axes(value, axes, turns, dim):
    return joined_along(all_blocks(value, axes, turns), dim)


def normalize(values, gain_term, shift_term):
    average = jnp.mean(values, axis=-1, keepdims=True)
    centred = values - average
    variance = jnp.mean(centred * centred, axis=-1, keepdims=True)
    return centred * lax.rsqrt(variance + epsilon) * gain_term + shift_term


def level_update(nodes, edges, sender_terms, senders, weights):
    (
        self_matrix,
        receiver_matrix,
        edge_bias,
        edge_output,
        edge_gain,
        edge_shift,
        node_self,
        node_summed,
        node_bias,
        node_output,
        node_gain,
        node_shift,
    ) = weights
    fanout, height, breadth, feature = edges.shape
    places = height * breadth
    flat_nodes = nodes.reshape(places, feature)
    flat_edges = edges.reshape(fanout * places, feature)
    receiver = jnp.dot(flat_nodes, receiver_matrix, preferred_element_type=jnp.float32) + edge_bias
    latent = jnp.dot(flat_edges, self_matrix, preferred_element_type=jnp.float32).reshape(
        fanout, places, -1
    )
    latent = (
        latent + jnp.take(sender_terms, senders.reshape(fanout, places), axis=0) + receiver[None]
    )
    hidden = jax.nn.silu(latent).astype(jnp.bfloat16).reshape(fanout * places, -1)
    message = jnp.dot(hidden, edge_output, preferred_element_type=jnp.float32)
    new_edges = (flat_edges.astype(jnp.float32) + normalize(message, edge_gain, edge_shift)).astype(
        jnp.bfloat16
    )
    new_edges = new_edges.reshape(fanout, places, feature)
    summed = jnp.sum(new_edges.astype(jnp.float32), axis=0).astype(jnp.bfloat16)
    node_hidden = jnp.dot(flat_nodes, node_self, preferred_element_type=jnp.float32)
    node_hidden = (
        node_hidden + jnp.dot(summed, node_summed, preferred_element_type=jnp.float32) + node_bias
    )
    node_hidden = jax.nn.silu(node_hidden).astype(jnp.bfloat16)
    node_message = jnp.dot(node_hidden, node_output, preferred_element_type=jnp.float32)
    new_nodes = (
        flat_nodes.astype(jnp.float32) + normalize(node_message, node_gain, node_shift)
    ).astype(jnp.bfloat16)
    return (
        new_nodes.reshape(height, breadth, feature),
        new_edges.reshape(fanout, height, breadth, feature),
    )


def offset_index(link_codes, reach_cells, padded_breadth):
    window_span = 2 * reach_cells + 1
    row_place = lax.broadcasted_iota(jnp.int32, link_codes.shape, 1)
    col_place = lax.broadcasted_iota(jnp.int32, link_codes.shape, 2)
    return (
        (row_place + link_codes // window_span) * padded_breadth
        + col_place
        + link_codes % window_span
    )


def widen(parent_values, height, breadth):
    parent_rows, parent_cols, feature = parent_values.shape
    spread_out = jnp.broadcast_to(
        parent_values[:, None, :, None, :], (parent_rows, 4, parent_cols, 4, feature)
    )
    return spread_out.reshape(height, breadth, feature)


def assemble_nodes(pieces, across, along):
    total, block_rows, block_cols, feature = pieces.shape
    arranged = pieces.reshape(across, along, block_rows, block_cols, feature).transpose(
        0, 2, 1, 3, 4
    )
    return arranged.reshape(across * block_rows, along * block_cols, feature)


def per_device(
    fine_nodes,
    fine_edges,
    fine_links,
    mid_nodes,
    mid_edges,
    mid_links,
    coarse_nodes,
    coarse_edges,
    coarse_links,
    edge_self,
    edge_sender,
    edge_receiver,
    edge_bias,
    edge_output,
    edge_gain,
    edge_shift,
    node_self,
    node_summed,
    node_bias,
    node_output,
    node_gain,
    node_shift,
    prolongation,
    pooling,
):
    tile_rows, tile_cols, feature = fine_nodes.shape
    mid_rows, mid_cols = (tile_rows // 4, tile_cols // 4)
    block_rows, block_cols = (tile_rows // 16, tile_cols // 16)
    coarse_rows, coarse_cols = (coarse_nodes.shape[0], coarse_nodes.shape[1])
    across = lax.axis_size(DX)
    along = lax.axis_size(DY)
    first_index = lax.axis_index(DX)
    second_index = lax.axis_index(DY)
    row_offset = first_index * block_rows
    col_offset = second_index * block_cols
    zero_offset = jnp.zeros((), jnp.int32)
    weights = tuple(
        (
            stacked[0]
            for stacked in (
                edge_self,
                edge_receiver,
                edge_bias,
                edge_output,
                edge_gain,
                edge_shift,
                node_self,
                node_summed,
                node_bias,
                node_output,
                node_gain,
                node_shift,
            )
        )
    )
    sender_matrix = edge_sender[0]
    fine_rim = with_halo(fine_nodes, ((DX, 0), (DY, 1)), FINE_REACH)
    fine_terms = jnp.dot(
        fine_rim.reshape(-1, feature), sender_matrix, preferred_element_type=jnp.float32
    )
    fine_index = offset_index(fine_links, FINE_REACH, tile_cols + 2 * FINE_REACH)
    fine_new, fine_edges = level_update(fine_nodes, fine_edges, fine_terms, fine_index, weights)
    pooled = (
        mid_nodes.astype(jnp.float32)
        .reshape(block_rows, 4, block_cols, 4, feature)
        .mean(axis=(1, 3))
        .astype(jnp.bfloat16)
    )
    raised = jnp.dot(pooled.reshape(-1, feature), pooling[0], preferred_element_type=jnp.float32)
    own_coarse = lax.dynamic_slice(
        coarse_nodes, (row_offset, col_offset, zero_offset), (block_rows, block_cols, feature)
    )
    own_coarse = (
        own_coarse.astype(jnp.float32) + raised.reshape(block_rows, block_cols, feature)
    ).astype(jnp.bfloat16)
    gathered = gather_axes(own_coarse[None], (("dx_0", "dx_1", "dy_0", "dy_1"), "dy_2"), (0, 1), 0)
    coarse_nodes = assemble_nodes(gathered, across, along)
    coarse_terms = jnp.dot(
        coarse_nodes.reshape(-1, feature), sender_matrix, preferred_element_type=jnp.float32
    )
    coarse_nodes, coarse_edges = level_update(
        coarse_nodes, coarse_edges, coarse_terms, coarse_links, weights
    )
    lifted = jnp.dot(
        coarse_nodes.reshape(-1, feature), prolongation[0], preferred_element_type=jnp.float32
    )
    lifted = lifted.reshape(coarse_rows, coarse_cols, feature)
    mid_source = mid_nodes
    mid_rim = with_halo(mid_source, ((DX, 0), (DY, 1)), MID_REACH)
    row_places = (
        first_index * mid_rows - MID_REACH + jnp.arange(mid_rows + 2 * MID_REACH, dtype=jnp.int32)
    )
    col_places = (
        second_index * mid_cols - MID_REACH + jnp.arange(mid_cols + 2 * MID_REACH, dtype=jnp.int32)
    )
    row_parent = row_places % (coarse_rows * 4) // 4
    col_parent = col_places % (coarse_cols * 4) // 4
    rim_lift = jnp.take(jnp.take(lifted, row_parent, axis=0), col_parent, axis=1)
    mid_rim = (mid_rim.astype(jnp.float32) + rim_lift).astype(jnp.bfloat16)
    mid_nodes = mid_rim[MID_REACH : MID_REACH + mid_rows, MID_REACH : MID_REACH + mid_cols]
    mid_terms = jnp.dot(
        mid_rim.reshape(-1, feature), sender_matrix, preferred_element_type=jnp.float32
    )
    mid_index = offset_index(mid_links, MID_REACH, mid_cols + 2 * MID_REACH)
    mid_nodes, mid_edges = level_update(mid_nodes, mid_edges, mid_terms, mid_index, weights)
    lifted_mid = jnp.dot(
        mid_nodes.reshape(-1, feature), prolongation[0], preferred_element_type=jnp.float32
    )
    lifted_mid = lifted_mid.reshape(mid_rows, mid_cols, feature)
    fine_nodes = (fine_new.astype(jnp.float32) + widen(lifted_mid, tile_rows, tile_cols)).astype(
        jnp.bfloat16
    )
    return (fine_nodes, fine_edges, mid_nodes, mid_edges, coarse_nodes, coarse_edges)


def solution(mesh):
    torus = Mesh(mesh.devices.reshape(2, 4, 2, 4, 2), ("dx_0", "dx_1", "dy_0", "dy_1", "dy_2"))
    in_specs = (
        P(DX, DY, None),
        P(None, DX, DY, None),
        P(None, DX, DY),
        P(DX, DY, None),
        P(None, DX, DY, None),
        P(None, DX, DY),
        P(),
        P(),
        P(),
        P(),
        P(),
        P(),
        P(),
        P(),
        P(),
        P(),
        P(),
        P(),
        P(),
        P(),
        P(),
        P(),
        P(),
        P(),
    )
    out_specs = (
        P(DX, DY, None),
        P(None, DX, DY, None),
        P(DX, DY, None),
        P(None, DX, DY, None),
        P(),
        P(),
    )
    return jax.shard_map(
        per_device, mesh=torus, in_specs=in_specs, out_specs=out_specs, check_vma=False
    )
```

profile of v0, /device:TPU:0, one launch (start us, length us, event | category | flops | bytes accessed | tf_op | source)
XLA Modules:
  0.0 355.0 jit_solution(18027557386560085851)
XLA Ops:
  0.6 1.6 fusion.84
  2.2 1.6 collective-permute-start
  3.8 2.5 collective-permute-start.1
  6.4 0.8 copy.115
  7.8 4.1 %collective-permute-start.5 = (bf16[1,4,512]{2,0,1:T(2,128)(2,1)}, bf16[1,4,512]{2,0,1:T(2,128)(2,1)}, u32[]{:S(2)}, u32[]{:S(2)}) collective-permute-start(bf16[1,4,512]{2,0,1:T(2,128)(2,1)} %get-tuple-element.13), channel_id=1, source_target_pairs={{16,0},{32,16},{48,32},{64,48},{80,64},{96,80},{112,96},{0,112},{1... | collective-permute-start | bytes 12296 | tf_op jit(solution)/shard_map/ppermute | solution.py:24
  11.9 0.9 fusion.67
  12.8 0.7 reshape.525
  13.6 0.7 reshape.523
  14.3 0.8 convert_reduce_fusion
  15.1 1.5 reshape.531
  16.6 1.5 reshape.530
  18.1 0.7 constant_dynamic-slice_fusion
  18.8 1.2 fusion.44
  20.0 176.0 %all-gather = bf16[128,1,512]{2,1,0:T(2,128)(2,1)S(1)} all-gather(bf16[2,1,512]{2,1,0:T(2,128)(2,1)S(1)} %copy.119), channel_id=2, replica_groups=mesh['dx_0'=2,'dx_1'=4,'dy_0'=2,'dy_1'=4,'dy_2'=2] {'dx_0','dx_1','dy_0'..., dimensions={0}, use_global_device_ids=true | all-gather | bytes 133120 | tf_op jit(solution)/shard_map/all_gather | solution.py:38
  196.0 0.8 reduce.8
  196.9 2.2 all_gather.7
  199.5 3.9 %fusion.37 = f32[512,1536]{1,0:T(8,128)} fusion(bf16[512,512]{1,0:T(8,128)(2,1)} %bitcast.175, bf16[1,512,1536]{2,1,0:T(8,128)(2,1)S(1)} %copy-done.1), kind=kOutput, calls=%fused_computation.56 | convolution fusion | flops 805306368 | bytes 5242880 | tf_op jit(solution)/shard_map/dot_general | solution.py:89
  203.4 2.6 convolution_add_fusion.1
  206.0 1.7 convolution_add_fusion.3
  207.7 1.7 fusion.35
  211.1 2.0 fusion.26
  213.2 6.7 %gather_fusion.1 = f32[1536,1536]{1,0:T(8,128)} fusion(f32[256,1536]{1,0:T(8,128)S(1)} %fusion.26, s32[2048]{0:T(1024)S(1)} %pad_clamp_fusion), kind=kCustom, calls=%fused_computation.1 | custom fusion | bytes 18880512 | tf_op jit(solution)/shard_map/jit(_take)/gather | solution.py:80
  219.9 7.3 %multiply_convert_fusion.1 = bf16[6,256,1536]{2,1,0:T(8,128)(2,1)S(1)} fusion(f32[6,256,1536]{2,1,0:T(8,128)} %bitcast.169, bf16[6,256,512]{2,1,0:T(8,128)(2,1)} %bitcast.180, f32[256,1536]{1,0:T(8,128)} %convolution_add_fusion.3, pred[6,256]{1,0:T(8,128)(4,1)S(1)} %compare_and_fusion.1, bf16[1,512,1536]{2,1,0:T(8,128)(2,1)S(1)} %copy-done), kind=kOutput, calls=%fused_computation.6 | convolution fusion | flops 2434793472 | bytes 18875904 | tf_op jit(solution)/shard_map/dot_general | solution.py:76
  227.2 2.7 fusion.86
  230.5 0.7 copy-done.16
  231.3 1.1 fusion.2
  232.4 1.2 reduce_sum.170
  233.6 4.4 %fusion.87 = (f32[256]{0:T(256)S(1)}, f32[256,512]{1,0:T(8,128)}) fusion(bf16[1,1536,512]{2,1,0:T(8,128)(2,1)} %param.43, f32[256,1536]{1,0:T(8,128)} %fusion.35, bf16[256,512]{1,0:T(8,128)(2,1)} %reduce_sum.170, bf16[1,512,1536]{2,1,0:T(8,128)(2,1)} %param.41, f32[1536]{0:T(1024)S(1)} %reduce.7), kind=kOutput, calls=%fused_computation.187 | convolution fusion | flops 808189696 | bytes 5512192 | tf_op jit(solution)/shard_map/dot_general | solution.py:94
  237.9 1.3 multiply_reduce_fusion.3
  239.9 1.2 add_convert_fusion.1
  243.3 1.3 pad_maximum_fusion.3
  244.8 5.2 %collective-permute-start.7 = (bf16[10,1,512]{2,0,1:T(8,128)(2,1)}, bf16[10,1,512]{2,0,1:T(8,128)(2,1)}, u32[]{:S(2)}, u32[]{:S(2)}) collective-permute-start(bf16[10,1,512]{2,0,1:T(8,128)(2,1)} %get-tuple-element.11), channel_id=1, source_target_pairs={{1,0},{2,1},{3,2},{4,3},{5,4},{6,5},{7,6},{8,7},{9,8},{10,9},{11,1... | collective-permute-start | bytes 30728 | tf_op jit(solution)/shard_map/ppermute | solution.py:24
  250.6 0.7 dot_general.100
  251.4 1.0 copy.124
  252.4 2.5 gather_fusion.3
  254.9 1.0 fusion.57
  255.9 0.7 copy.127
  257.3 1.4 reshape.534
  258.7 2.5 convolution_add_fusion.6
  261.2 1.1 fusion.33
  262.2 0.9 convert_element_type.146
  263.1 1.8 fusion.24
  264.9 1.1 gather_fusion.4
  266.0 1.7 multiply_convert_fusion.4
  268.9 2.7 fusion.91
  272.0 0.8 constant_dynamic-update-slice_fusion.2
  272.8 0.8 constant_dynamic-update-slice_fusion
  273.6 0.8 copy-done.17
  274.5 0.8 fusion.83
  275.3 5.4 %collective-permute-start.3 = (bf16[38,3,512]{2,1,0:T(4,128)(2,1)}, bf16[38,3,512]{2,1,0:T(4,128)(2,1)S(1)}, u32[]{:S(2)}, u32[]{:S(2)}) collective-permute-start(bf16[38,3,512]{2,1,0:T(4,128)(2,1)} %get-tuple-element.7), channel_id=1, source_target_pairs={{1,0},{2,1},{3,2},{4,3},{5,4},{6,5},{7,6},{8,7},{9,8},{10,9},{11,1... | collective-permute-start | bytes 350216 | tf_op jit(solution)/shard_map/ppermute | solution.py:24
  280.9 0.7 reshape_reshape.15
  281.8 1.3 reshape.540
  283.8 2.6 pad_maximum_fusion
  286.3 2.1 reshape.524
  288.5 5.0 %fusion.28 = f32[836,1536]{1,0:T(8,128)} fusion(bf16[836,512]{1,0:T(8,128)(2,1)} %reshape.524, bf16[1,512,1536]{2,1,0:T(8,128)(2,1)S(1)} %copy-done.4), kind=kOutput, calls=%fused_computation.47 | convolution fusion | flops 1314914304 | bytes 7565312 | tf_op jit(solution)/shard_map/dot_general | solution.py:189
  293.5 23.1 %gather_fusion = f32[3072,1536]{1,0:T(8,128)} fusion(f32[836,1536]{1,0:T(8,128)} %fusion.28, s32[3072]{0:T(1024)S(1)} %copy-done.26), kind=kCustom, calls=%fused_computation | custom fusion | bytes 37761024 | tf_op jit(solution)/shard_map/jit(_take)/gather | solution.py:80
  316.6 14.7 %multiply_convert_fusion = bf16[6,512,1536]{2,1,0:T(8,128)(2,1)} fusion(f32[6,512,1536]{2,1,0:T(8,128)} %bitcast.166, f32[512,1536]{1,0:T(8,128)} %convolution_add_fusion.1, pred[6,512]{1,0:T(8,128)(4,1)S(1)} %copy-done.43, bf16[6,512,512]{2,1,0:T(8,128)(2,1)} %bitcast.177, bf16[1,512,1536]{2,1,0:T(8,128)(2,1)S(1)} %copy-done), kind=kOutput, calls=%fused_computation.5 | convolution fusion | flops 4869586944 | bytes 36178944 | tf_op jit(solution)/shard_map/dot_general | solution.py:76
  331.3 7.9 %fusion.94 = (f32[3072]{0:T(1024)S(1)}, f32[3072,512]{1,0:T(8,128)S(1)}) fusion(bf16[3072,1536]{1,0:T(8,128)(2,1)} %bitcast.200, bf16[1,1536,512]{2,1,0:T(8,128)(2,1)S(1)} %copy-done.15), kind=kOutput, calls=%fused_computation.190 | convolution fusion | flops 4833408000 | bytes 17313792 | tf_op jit(solution)/shard_map/dot_general | solution.py:83
  339.2 2.1 multiply_reduce_fusion
  341.4 3.0 fusion
  344.4 3.3 reduce_sum.162
  347.7 5.1 %fusion.95 = (f32[512]{0:T(512)S(1)}, f32[512,512]{1,0:T(8,128)S(1)}) fusion(bf16[1,1536,512]{2,1,0:T(8,128)(2,1)} %param.43, f32[512,1536]{1,0:T(8,128)} %fusion.37, bf16[512,512]{1,0:T(8,128)(2,1)} %reduce_sum.162, bf16[1,512,1536]{2,1,0:T(8,128)(2,1)} %param.41, f32[1536]{0:T(1024)S(1)} %reduce.7), kind=kOutput, calls=%fused_computation.191 | convolution fusion | flops 1616379392 | bytes 7872512 | tf_op jit(solution)/shard_map/dot_general | solution.py:94
  353.4 0.6 copy-done.9
  354.1 1.0 fusion.45
  (161 shorter events, 10.7 us)
Async XLA Ops:
  0.6 219.2 %copy-start = (bf16[1,512,1536]{2,1,0:T(8,128)(2,1)S(1)}, bf16[1,512,1536]{2,1,0:T(8,128)(2,1)}, u32[]{:S(2)}) copy-start(bf16[1,512,1536]{2,1,0:T(8,128)(2,1)} %param.33) | copy-start | bytes 4718596
  2.2 269.7 %collective-permute-start = (bf16[3,16,512]{2,1,0:T(8,128)(2,1)}, bf16[3,16,512]{2,1,0:T(8,128)(2,1)}, u32[]{:S(2)}, u32[]{:S(2)}) collective-permute-start(bf16[3,16,512]{2,1,0:T(8,128)(2,1)} %get-tuple-element.9), channel_id=1, source_target_pairs={{0,16},{16,32},{32,48},{48,64},{64,80},{80,96},{96,112},{112,0},{1... | collective-permute-start | bytes 147464 | tf_op jit(solution)/shard_map/ppermute | solution.py:23
  3.8 269.0 %collective-permute-start.1 = (bf16[3,16,512]{2,1,0:T(8,128)(2,1)}, bf16[3,16,512]{2,1,0:T(8,128)(2,1)}, u32[]{:S(2)}, u32[]{:S(2)}) collective-permute-start(bf16[3,16,512]{2,1,0:T(8,128)(2,1)} %get-tuple-element.8), channel_id=1, source_target_pairs={{16,0},{32,16},{48,32},{64,48},{80,64},{96,80},{112,96},{0,112},{1... | collective-permute-start | bytes 147464 | tf_op jit(solution)/shard_map/ppermute | solution.py:24
  7.1 4.8 %copy-start.23 = (bf16[8,4,512]{2,0,1:T(8,128)(2,1)}, bf16[8,4,512]{2,0,1:T(8,128)(2,1)S(1)}, u32[]{:S(2)}) copy-start(bf16[8,4,512]{2,0,1:T(8,128)(2,1)S(1)} %copy.115) | copy-start | bytes 98308
  7.8 235.6 %collective-permute-start.4 = (bf16[1,4,512]{2,0,1:T(2,128)(2,1)}, bf16[1,4,512]{2,0,1:T(2,128)(2,1)}, u32[]{:S(2)}, u32[]{:S(2)}) collective-permute-start(bf16[1,4,512]{2,0,1:T(2,128)(2,1)} %get-tuple-element.12), channel_id=1, source_target_pairs={{0,16},{16,32},{32,48},{48,64},{64,80},{80,96},{96,112},{112,0},{1... | collective-permute-start | bytes 12296 | tf_op jit(solution)/shard_map/ppermute | solution.py:23
  7.8 235.6 %collective-permute-start.5 = (bf16[1,4,512]{2,0,1:T(2,128)(2,1)}, bf16[1,4,512]{2,0,1:T(2,128)(2,1)}, u32[]{:S(2)}, u32[]{:S(2)}) collective-permute-start(bf16[1,4,512]{2,0,1:T(2,128)(2,1)} %get-tuple-element.13), channel_id=1, source_target_pairs={{16,0},{32,16},{48,32},{64,48},{80,64},{96,80},{112,96},{0,112},{1... | collective-permute-start | bytes 12296 | tf_op jit(solution)/shard_map/ppermute | solution.py:24
  20.0 179.4 %copy-start.41 = (f32[1,1536]{1,0:T(1,128)S(1)}, f32[1,1536]{1,0:T(1,128)}, u32[]{:S(2)}) copy-start(f32[1,1536]{1,0:T(1,128)} %param.36) | copy-start | bytes 18436
  20.0 179.4 %copy-start.1 = (bf16[1,512,1536]{2,1,0:T(8,128)(2,1)S(1)}, bf16[1,512,1536]{2,1,0:T(8,128)(2,1)}, u32[]{:S(2)}) copy-start(bf16[1,512,1536]{2,1,0:T(8,128)(2,1)} %param.40) | copy-start | bytes 4718596
  199.4 3.9 %copy-start.3 = (bf16[1,512,1536]{2,1,0:T(8,128)(2,1)S(1)}, bf16[1,512,1536]{2,1,0:T(8,128)(2,1)}, u32[]{:S(2)}) copy-start(bf16[1,512,1536]{2,1,0:T(8,128)(2,1)} %param.35) | copy-start | bytes 4718596
  199.4 3.9 %copy-start.6 = (bf16[32,16,512]{2,1,0:T(8,128)(2,1)S(1)}, bf16[32,16,512]{2,1,0:T(8,128)(2,1)}, u32[]{:S(2)}) copy-start(bf16[32,16,512]{2,1,0:T(8,128)(2,1)} %param.24) | copy-start | bytes 1572868
  207.7 1.8 copy-start.40
  207.7 2.1 copy-start.28
  207.7 2.7 copy-start.27
  207.7 3.3 copy-start.42
  211.1 2.0 copy-start.30
  211.1 2.1 copy-start.29
  219.9 7.3 %copy-start.13 = (bf16[1,1536,512]{2,1,0:T(8,128)(2,1)S(1)}, bf16[1,1536,512]{2,1,0:T(8,128)(2,1)}, u32[]{:S(2)}) copy-start(bf16[1,1536,512]{2,1,0:T(8,128)(2,1)} %param.37) | copy-start | bytes 4718596
  229.9 1.4 copy-start.16
  229.9 1.4 copy-start.31
  229.9 1.4 copy-start.33
  232.3 5.6 %copy-start.5 = (bf16[1536,512]{1,0:T(8,128)(2,1)}, bf16[1536,512]{1,0:T(8,128)(2,1)S(1)}, u32[]{:S(2)}) copy-start(bf16[1536,512]{1,0:T(8,128)(2,1)S(1)} %fusion.2) | copy-start | bytes 4718596
  233.5 6.3 %copy-start.35 = (f32[1,512]{1,0:T(1,128)S(1)}, f32[1,512]{1,0:T(1,128)}, u32[]{:S(2)}) copy-start(f32[1,512]{1,0:T(1,128)} %param.45) | copy-start | bytes 6148
  233.5 6.3 %copy-start.37 = (f32[1,512]{1,0:T(1,128)S(1)}, f32[1,512]{1,0:T(1,128)}, u32[]{:S(2)}) copy-start(f32[1,512]{1,0:T(1,128)} %param.44) | copy-start | bytes 6148
  237.9 3.2 copy-start.11
  241.1 1.0 copy-start.18
  241.1 2.2 copy-start.24
  241.1 9.5 %copy-start.20 = (bf16[6,8,4,512]{3,2,1,0:T(4,128)(2,1)S(1)}, bf16[6,8,4,512]{3,2,1,0:T(4,128)(2,1)}, u32[]{:S(2)}) copy-start(bf16[6,8,4,512]{3,2,1,0:T(4,128)(2,1)} %param.28) | copy-start | bytes 589828
  244.7 10.2 %collective-permute-start.6 = (bf16[10,1,512]{2,0,1:T(8,128)(2,1)}, bf16[10,1,512]{2,0,1:T(8,128)(2,1)}, u32[]{:S(2)}, u32[]{:S(2)}) collective-permute-start(bf16[10,1,512]{2,0,1:T(8,128)(2,1)} %get-tuple-element.10), channel_id=1, source_target_pairs={{0,1},{1,2},{2,3},{3,4},{4,5},{5,6},{6,7},{7,8},{8,9},{9,10},{10,1... | collective-permute-start | bytes 30728 | tf_op jit(solution)/shard_map/ppermute | solution.py:23
  244.8 10.1 %collective-permute-start.7 = (bf16[10,1,512]{2,0,1:T(8,128)(2,1)}, bf16[10,1,512]{2,0,1:T(8,128)(2,1)}, u32[]{:S(2)}, u32[]{:S(2)}) collective-permute-start(bf16[10,1,512]{2,0,1:T(8,128)(2,1)} %get-tuple-element.11), channel_id=1, source_target_pairs={{1,0},{2,1},{3,2},{4,3},{5,4},{6,5},{7,6},{8,7},{9,8},{10,9},{11,1... | collective-permute-start | bytes 30728 | tf_op jit(solution)/shard_map/ppermute | solution.py:24
  252.4 8.7 %copy-start.2 = (bf16[1,512,1536]{2,1,0:T(8,128)(2,1)S(1)}, bf16[1,512,1536]{2,1,0:T(8,128)(2,1)}, u32[]{:S(2)}) copy-start(bf16[1,512,1536]{2,1,0:T(8,128)(2,1)} %param.40) | copy-start | bytes 4718596
  258.7 2.5 copy-start.21
  261.1 3.8 %copy-start.39 = (s32[1024]{0:T(1024)S(1)}, s32[1024]{0:T(1024)}, u32[]{:S(2)}) copy-start(s32[1024]{0:T(1024)} %get-tuple-element.26) | copy-start | bytes 12292
  264.9 1.1 copy-start.44
  266.0 1.8 copy-start.14
  267.7 0.9 copy-start.32
  267.8 0.8 copy-start.34
  267.8 1.0 copy-start.19
  268.8 3.0 copy-start.22
  268.8 3.0 copy-start.36
  268.8 3.0 copy-start.38
  268.9 3.9 %copy-start.7 = (bf16[32,16,512]{2,1,0:T(8,128)(2,1)S(1)}, bf16[32,16,512]{2,1,0:T(8,128)(2,1)}, u32[]{:S(2)}) copy-start(bf16[32,16,512]{2,1,0:T(8,128)(2,1)} %param.24) | copy-start | bytes 1572868
  271.6 9.1 %copy-start.12 = (bf16[1,512,512]{2,1,0:T(8,128)(2,1)S(1)}, bf16[1,512,512]{2,1,0:T(8,128)(2,1)}, u32[]{:S(2)}) copy-start(bf16[1,512,512]{2,1,0:T(8,128)(2,1)} %param.46) | copy-start | bytes 1572868
  271.9 9.9 %copy-start.25 = (bf16[8,4,512]{2,1,0:T(4,128)(2,1)}, bf16[8,4,512]{2,1,0:T(4,128)(2,1)S(1)}, u32[]{:S(2)}) copy-start(bf16[8,4,512]{2,1,0:T(4,128)(2,1)S(1)} %reshape.539) | copy-start | bytes 98308
  273.6 0.8 copy-start.17
  275.3 8.5 %collective-permute-start.2 = (bf16[38,3,512]{2,1,0:T(4,128)(2,1)}, bf16[38,3,512]{2,1,0:T(4,128)(2,1)S(1)}, u32[]{:S(2)}, u32[]{:S(2)}) collective-permute-start(bf16[38,3,512]{2,1,0:T(4,128)(2,1)} %get-tuple-element.6), channel_id=1, source_target_pairs={{0,1},{1,2},{2,3},{3,4},{4,5},{5,6},{6,7},{7,8},{8,9},{9,10},{10,1... | collective-permute-start | bytes 350216 | tf_op jit(solution)/shard_map/ppermute | solution.py:23
  275.3 8.5 %collective-permute-start.3 = (bf16[38,3,512]{2,1,0:T(4,128)(2,1)}, bf16[38,3,512]{2,1,0:T(4,128)(2,1)S(1)}, u32[]{:S(2)}, u32[]{:S(2)}) collective-permute-start(bf16[38,3,512]{2,1,0:T(4,128)(2,1)} %get-tuple-element.7), channel_id=1, source_target_pairs={{1,0},{2,1},{3,2},{4,3},{5,4},{6,5},{7,6},{8,7},{9,8},{10,9},{11,1... | collective-permute-start | bytes 350216 | tf_op jit(solution)/shard_map/ppermute | solution.py:24
  283.2 5.3 %copy-start.4 = (bf16[1,512,1536]{2,1,0:T(8,128)(2,1)S(1)}, bf16[1,512,1536]{2,1,0:T(8,128)(2,1)}, u32[]{:S(2)}) copy-start(bf16[1,512,1536]{2,1,0:T(8,128)(2,1)} %param.34) | copy-start | bytes 4718596
  288.5 5.0 %copy-start.26 = (s32[3072]{0:T(1024)S(1)}, s32[3072]{0:T(1024)}, u32[]{:S(2)}) copy-start(s32[3072]{0:T(1024)} %broadcast_clamp_fusion) | copy-start | bytes 36868
  293.5 23.1 %copy-start.43 = (pred[6,512]{1,0:T(8,128)(4,1)S(1)}, pred[6,512]{1,0:T(8,128)(4,1)}, u32[]{:S(2)}) copy-start(pred[6,512]{1,0:T(8,128)(4,1)} %compare_and_fusion) | copy-start | bytes 9220
  316.6 14.7 %copy-start.15 = (bf16[1,1536,512]{2,1,0:T(8,128)(2,1)S(1)}, bf16[1,1536,512]{2,1,0:T(8,128)(2,1)}, u32[]{:S(2)}) copy-start(bf16[1,1536,512]{2,1,0:T(8,128)(2,1)} %param.37) | copy-start | bytes 4718596
  339.2 2.1 copy-start.10
  347.7 5.4 %copy-start.8 = (bf16[32,16,512]{2,1,0:T(8,128)(2,1)S(1)}, bf16[32,16,512]{2,1,0:T(8,128)(2,1)}, u32[]{:S(2)}) copy-start(bf16[32,16,512]{2,1,0:T(8,128)(2,1)} %param.24) | copy-start | bytes 1572868
  352.8 1.2 copy-start.9
where the time goes:
time: 356 us; the launch traced here: 355 us
  blocking collectives  178 us (50%)
  matrix products  71 us (20%)
  local copies, waits for them, and re-layouts  57.6 us (16%)
  other arithmetic  27.2 us (8%)
  starting transfers between devices  19 us (5%)
    all_gather x2, blocking collectives, all_blocks(): blocks = lax.all_gather(blocks, axes[k], axis=0, tiled=True)  178 us
    gather x3, local copies, waits for them, and re-layouts, level_update(): jnp.take(sender_terms, senders.reshape(fanout, places), axis=0)  30.9 us
    dot_general x3, matrix products, level_update(): jnp.dot(flat_edges, self_matrix, preferred_element_type=jnp.float32)  23.7 us
    ppermute x4, starting transfers between devices, with_halo(): after = lax.ppermute(leading, axis, down)  17.2 us
    dot_general x3, matrix products, level_update(): jnp.dot(node_hidden, node_output, preferred_element_type=jnp.float32)  12.2 us
    dot_general x3, matrix products, level_update(): message = jnp.dot(hidden, edge_output, preferred_element_type=jnp.float32)  11.1 us
  transfers between devices with their start and end apart: 8, of which 1 were waited for; matrix products, arithmetic and copies ran while one was open for 22% of the time, Pallas kernels for 0%

commit v1 on v0

v1 whole, which is shorter than its diff:
```python
import functools

import jax
import jax.numpy as jnp
from jax import lax
from jax.experimental import pallas as pl
from jax.experimental.pallas import tpu as pltpu
from jax.sharding import PartitionSpec as P

EPS = 1e-05
BF = jnp.bfloat16
F32 = jnp.float32
MIB = 1 << 20


def dot(a, b):
    return jnp.dot(a, b, preferred_element_type=F32)


def onehot_rows(index_row, width):
    down = jnp.broadcast_to(index_row, (128, 128)).T
    lane = lax.broadcasted_iota(jnp.int32, (128, 128), 1)
    parts = [(down == lane + base).astype(F32).astype(BF) for base in range(0, width, 128)]
    return parts[0] if len(parts) == 1 else jnp.concatenate(parts, axis=1)


def norm(values, gain, shift):
    centred = values - jnp.mean(values, axis=-1, keepdims=True)
    variance = jnp.mean(centred * centred, axis=-1, keepdims=True)
    return centred * lax.rsqrt(variance + EPS) * gain + shift


def silu_of_half(half):
    return (half + half * jnp.tanh(half)).astype(BF)


CHUNK = 256


def sender_and_receiver(nodes_send, nodes_recv, w, table, recv):
    hidden = w.sender.shape[1]
    for n in range(0, hidden, CHUNK):
        cols = slice(n, n + CHUNK)
        table[0 : nodes_send.shape[0], cols] = (0.5 * dot(nodes_send, w.sender[:, cols])).astype(BF)
        recv[0 : nodes_recv.shape[0], cols] = 0.5 * (
            dot(nodes_recv, w.receiver[:, cols]) + w.bias[:, cols]
        )


def edge_block(edges, first_row, places, w, lhs, rhs, act, recv):
    rows, feature = edges.shape
    hidden = rhs.shape[1]
    lhs[0:rows, 0:feature] = edges
    for n in range(0, hidden, CHUNK):
        cols = slice(n, n + CHUNK)
        half = dot(lhs[0:rows, :], rhs[:, cols]).reshape(6, places, CHUNK)
        half = half + recv[pl.ds(first_row, places), cols][None]
        act[0:rows, cols] = silu_of_half(half).reshape(rows, CHUNK)
    message = dot(act[0:rows, :], w.output[...])
    new = (edges.astype(F32) + norm(message, w.gain[...], w.shift[...])).astype(BF)
    new = new.reshape(6, places, feature)
    total = new[0].astype(F32)
    for k in range(1, 6):
        total = total + new[k].astype(F32)
    return new, total.astype(BF)


def node_update(nodes, summed, w, act):
    rows = nodes.shape[0]
    hidden = w.node_self.shape[1]
    for n in range(0, hidden, CHUNK):
        cols = slice(n, n + CHUNK)
        half = 0.5 * (
            dot(nodes, w.node_self[:, cols])
            + dot(summed, w.node_summed[:, cols])
            + w.node_bias[:, cols]
        )
        act[0:rows, cols] = silu_of_half(half)
    message = dot(act[0:rows, :], w.node_output[...])
    return (nodes.astype(F32) + norm(message, w.node_gain[...], w.node_shift[...])).astype(BF)


class Weights:
    names = (
        "self", "sender", "receiver", "bias", "output", "gain", "shift",
        "node_self", "node_summed", "node_bias", "node_output", "node_gain", "node_shift",
    )

    def __init__(self, refs):
        for name, ref in zip(self.names, refs):
            setattr(self, name, ref)


COUNT = len(Weights.names)
WINDOW = 256


def load_self(w, rhs):
    rhs[0 : w.self.shape[0], :] = w.self[...] * jnp.asarray(0.5, BF)


def fine_kernel(stride, rim, nodes, index, edges, *refs):
    w = Weights(refs[:COUNT])
    new_nodes, new_edges = refs[COUNT : COUNT + 2]
    table, recv, lhs, rhs, act, summed = refs[COUNT + 2 :]
    step = pl.program_id(0)
    feature = nodes.shape[1]
    places = edges.shape[1]

    @pl.when(step == 0)
    def _():
        load_self(w, rhs)
        sender_and_receiver(rim[...], nodes[...], w, table, recv)

    for j in range(index.shape[1]):
        lhs[128 * j : 128 * j + 128, feature:] = onehot_rows(index[0, j : j + 1, :], WINDOW)
    base = pl.multiple_of(step * stride, 16)
    rhs[feature:, :] = table[pl.ds(base, WINDOW), :]
    first = pl.multiple_of(step * places, 16)
    block, total = edge_block(
        edges[...].reshape(6 * places, feature), first, places, w, lhs, rhs, act, recv
    )
    new_edges[...] = block
    summed[pl.ds(first, places), :] = total

    @pl.when(step == pl.num_programs(0) - 1)
    def _():
        new_nodes[...] = node_update(nodes[...], summed[...], w, act)


def coarse_mid_kernel(
    coarse_steps, mid_shape, coarse_shape, pooled, coarse, index, coarse_edges, mid_rim, parent, mid_index, mid_edges,
    fine, pooling, prolongation, *refs
):
    w = Weights(refs[:COUNT])
    coarse_out, coarse_edges_out, mid_out, mid_edges_out, fine_out = refs[COUNT : COUNT + 5]
    table, recv, lhs, rhs, act, summed, states = refs[COUNT + 5 :]
    step = pl.program_id(0)
    count, feature = coarse.shape
    places = coarse_edges.shape[1]

    @pl.when(step == 0)
    def _():
        load_self(w, rhs)
        block_rows, block_cols, grid_cols = coarse_shape
        place = lax.broadcasted_iota(jnp.int32, (count, count), 0)
        lane = lax.broadcasted_iota(jnp.int32, (count, count), 1)
        row, col = place // grid_cols, place % grid_cols
        device = (row // block_rows) * (grid_cols // block_cols) + col // block_cols
        source = (device * block_rows + row % block_rows) * block_cols + col % block_cols
        ordered = dot((lane == source).astype(F32).astype(BF), pooled[...]).astype(BF)
        before = coarse[...].astype(F32) + dot(ordered, pooling[...])
        states[...] = before.astype(BF)
        sender_and_receiver(states[...], states[...], w, table, recv)
        rhs[feature:, :] = table[...]

    @pl.when(step < coarse_steps)
    def _():
        for j in range(index.shape[1]):
            lhs[128 * j : 128 * j + 128, feature:] = onehot_rows(index[0, j : j + 1, :], WINDOW)
        first = pl.multiple_of(step * places, 16)
        block, total = edge_block(
            coarse_edges[...].reshape(6 * places, feature), first, places, w, lhs, rhs, act, recv
        )
        coarse_edges_out[...] = block
        summed[pl.ds(first, places), :] = total

    @pl.when(step == coarse_steps)
    def _():
        mid_rows, mid_cols = mid_shape
        mid_places = mid_rows * mid_cols
        updated = node_update(states[...], summed[...], w, act)
        coarse_out[...] = updated
        lifted = dot(
            dot(onehot_rows(parent[...], WINDOW), updated).astype(BF), prolongation[...]
        )
        rim = (mid_rim[...].astype(F32) + lifted).astype(BF)
        place = lax.broadcasted_iota(jnp.int32, (mid_places, 128), 0)
        lane = lax.broadcasted_iota(jnp.int32, (mid_places, 128), 1)
        inner = (place // mid_cols + 1) * (mid_cols + 2) + place % mid_cols + 1
        own = dot((lane == inner).astype(F32).astype(BF), rim).astype(BF)
        sender_and_receiver(rim, own, w, table, recv)
        rhs[feature : feature + 128, :] = table[0:128, :]
        rows = 6 * mid_places
        for j in range(mid_index.shape[0]):
            size = min(128, rows - 128 * j)
            hot = onehot_rows(mid_index[j : j + 1, :], WINDOW)
            lhs[128 * j : 128 * j + size, feature:] = hot[0:size]
        block, total = edge_block(mid_edges[...], 0, mid_places, w, lhs, rhs, act, recv)
        mid_edges_out[...] = block.reshape(rows, feature)
        mid_new = node_update(own, total, w, act)
        mid_out[...] = mid_new
        fine_rows = fine.shape[0]
        site = lax.broadcasted_iota(jnp.int32, (fine_rows, mid_places), 0)
        which = lax.broadcasted_iota(jnp.int32, (fine_rows, mid_places), 1)
        across = 4 * mid_cols
        over = (site // (4 * across)) * mid_cols + (site % across) // 4
        widened = dot((over == which).astype(F32).astype(BF), mid_new).astype(BF)
        fine_out[...] = (fine[...].astype(F32) + dot(widened, prolongation[...])).astype(BF)


def whole():
    return pl.BlockSpec(memory_space=pltpu.VMEM)


def run_fine(rim, nodes, index, edges, weights, stride):
    count, feature = nodes.shape
    hidden = weights[0].shape[1]
    steps = index.shape[0]
    places = count // steps
    return pl.pallas_call(
        functools.partial(fine_kernel, stride),
        grid=(steps,),
        in_specs=[
            whole(),
            whole(),
            pl.BlockSpec((1,) + index.shape[1:], lambda i: (i, 0, 0)),
            pl.BlockSpec((6, places, feature), lambda i: (0, i, 0)),
        ]
        + [whole()] * COUNT,
        out_specs=[whole(), pl.BlockSpec((6, places, feature), lambda i: (0, i, 0))],
        out_shape=[
            jax.ShapeDtypeStruct((count, feature), BF),
            jax.ShapeDtypeStruct((6, count, feature), BF),
        ],
        scratch_shapes=[
            pltpu.VMEM((rim.shape[0], hidden), BF),
            pltpu.VMEM((count, hidden), F32),
            pltpu.VMEM((6 * places, feature + WINDOW), BF),
            pltpu.VMEM((feature + WINDOW, hidden), BF),
            pltpu.VMEM((max(count, 6 * places), hidden), BF),
            pltpu.VMEM((count, feature), BF),
        ],
        compiler_params=pltpu.CompilerParams(
            dimension_semantics=("arbitrary",), vmem_limit_bytes=FINE_VMEM
        ),
        cost_estimate=pl.CostEstimate(
            flops=2 * 6 * count * (2 * feature + WINDOW) * hidden + 10 * count * feature * hidden,
            bytes_accessed=16 * MIB,
            transcendentals=7 * count * hidden,
        ),
        name="fine_level",
    )(rim, nodes, index, edges, *weights)


FINE_VMEM = 30 * MIB
COARSE_VMEM = 24 * MIB


def run_coarse_mid(
    pooled, coarse, index, coarse_edges, mid_rim, parent, mid_index, mid_edges, fine, pooling,
    prolongation, weights, mid_shape, coarse_shape
):
    count, feature = coarse.shape
    hidden = weights[0].shape[1]
    steps = index.shape[0]
    places = count // steps
    mid_places = mid_shape[0] * mid_shape[1]

    def at(i):
        return jnp.minimum(i, steps - 1)

    return pl.pallas_call(
        functools.partial(coarse_mid_kernel, steps, mid_shape, coarse_shape),
        grid=(steps + 1,),
        in_specs=[
            whole(),
            whole(),
            pl.BlockSpec((1,) + index.shape[1:], lambda i: (at(i), 0, 0)),
            pl.BlockSpec((6, places, feature), lambda i: (0, at(i), 0)),
        ]
        + [whole()] * (7 + COUNT),
        out_specs=[
            whole(),
            pl.BlockSpec((6, places, feature), lambda i: (0, at(i), 0)),
            whole(),
            whole(),
            whole(),
        ],
        out_shape=[
            jax.ShapeDtypeStruct((count, feature), BF),
            jax.ShapeDtypeStruct((6, count, feature), BF),
            jax.ShapeDtypeStruct((mid_places, feature), BF),
            jax.ShapeDtypeStruct((6 * mid_places, feature), BF),
            jax.ShapeDtypeStruct(fine.shape, BF),
        ],
        scratch_shapes=[
            pltpu.VMEM((WINDOW, hidden), BF),
            pltpu.VMEM((count, hidden), F32),
            pltpu.VMEM((6 * places, feature + WINDOW), BF),
            pltpu.VMEM((feature + WINDOW, hidden), BF),
            pltpu.VMEM((max(count, 6 * places), hidden), BF),
            pltpu.VMEM((count, feature), BF),
            pltpu.VMEM((count, feature), BF),
        ],
        compiler_params=pltpu.CompilerParams(
            dimension_semantics=("arbitrary",), vmem_limit_bytes=COARSE_VMEM
        ),
        cost_estimate=pl.CostEstimate(
            flops=2 * 6 * count * (2 * feature + WINDOW) * hidden + 10 * count * feature * hidden,
            bytes_accessed=8 * MIB,
            transcendentals=7 * count * hidden,
        ),
        name="coarse_mid_levels",
    )(
        pooled, coarse, index, coarse_edges, mid_rim, parent, mid_index, mid_edges, fine, pooling,
        prolongation, *weights
    )


def gather_coarse(pooled):
    devices = lax.axis_size("dx") * lax.axis_size("dy")
    own = pooled.reshape(-1, pooled.shape[-1])
    slots = jnp.broadcast_to(own[None], (devices,) + own.shape)
    received = lax.all_to_all(slots, ("dx", "dy"), 0, 0, tiled=True)
    return received.reshape(-1, own.shape[-1])


def per_device(
    fine_nodes, fine_edges, fine_links, mid_nodes, mid_edges, mid_links, coarse_nodes, coarse_edges,
    coarse_links, edge_self, edge_sender, edge_receiver, edge_bias, edge_output, edge_gain,
    edge_shift, node_self, node_summed, node_bias, node_output, node_gain, node_shift, prolongation,
    pooling,
):
    rows, cols, feature = fine_nodes.shape
    mid_rows, mid_cols = mid_nodes.shape[0], mid_nodes.shape[1]
    coarse_rows, coarse_cols = coarse_nodes.shape[0], coarse_nodes.shape[1]
    block_rows, block_cols = mid_rows // 4, mid_cols // 4
    weights = (
        edge_self[0], edge_sender[0], edge_receiver[0], edge_bias, edge_output[0], edge_gain,
        edge_shift, node_self[0], node_summed[0], node_bias, node_output[0], node_gain, node_shift,
    )
    pooled = (
        mid_nodes.astype(F32)
        .reshape(block_rows, 4, block_cols, 4, feature)
        .mean(axis=(1, 3))
        .astype(BF)
    )
    gathered = gather_coarse(pooled)

    def packed(fine_part, mid_part):
        return jnp.concatenate(
            [fine_part.reshape(-1, feature), mid_part.reshape(-1, feature)], axis=0
        )

    def exchange(fine, mid, axis, dim):
        count = lax.axis_size(axis)
        up = [(i, (i + 1) % count) for i in range(count)]
        down = [(j, i) for i, j in up]

        def edge(lo_fine, hi_fine, lo_mid, hi_mid):
            return (
                lax.slice_in_dim(fine, lo_fine, hi_fine, axis=dim),
                lax.slice_in_dim(mid, lo_mid, hi_mid, axis=dim),
            )

        fine_length, mid_length = fine.shape[dim], mid.shape[dim]
        last = edge(fine_length - 3, fine_length, mid_length - 1, mid_length)
        first = edge(0, 3, 0, 1)
        before = lax.ppermute(packed(*last), axis, up)
        after = lax.ppermute(packed(*first), axis, down)
        split = last[0].shape[0] * last[0].shape[1]

        def parted(rows_in):
            return rows_in[:split].reshape(last[0].shape), rows_in[split:].reshape(last[1].shape)

        (fine_before, mid_before), (fine_after, mid_after) = parted(before), parted(after)
        return (
            jnp.concatenate([fine_before, fine, fine_after], axis=dim),
            jnp.concatenate([mid_before, mid, mid_after], axis=dim),
        )

    fine_rim, mid_rim = exchange(fine_nodes, mid_nodes, "dx", 0)
    fine_rim, mid_rim = exchange(fine_rim, mid_rim, "dy", 1)
    width = 24
    fine_rim = jnp.pad(fine_rim, ((0, 0), (0, width - fine_rim.shape[1]), (0, 0)))
    fine_rim = jnp.pad(fine_rim.reshape(-1, feature), ((0, 16), (0, 0)))
    mid_rim = mid_rim.reshape(-1, feature)
    mid_rim = jnp.pad(mid_rim, ((0, 128 - mid_rim.shape[0]), (0, 0)))

    block = 4
    steps = rows // block
    r = lax.broadcasted_iota(jnp.int32, fine_links.shape, 1) % block
    c = lax.broadcasted_iota(jnp.int32, fine_links.shape, 2)
    fine_index = (r + fine_links // 7) * width + c + fine_links % 7
    fine_index = (
        fine_index.reshape(6, steps, block * cols).transpose(1, 0, 2).reshape(steps, -1, 128)
    )
    fine_new, fine_edges_new = run_fine(
        fine_rim,
        fine_nodes.reshape(-1, feature),
        fine_index,
        fine_edges.reshape(6, -1, feature),
        weights,
        block * width,
    )

    r = lax.broadcasted_iota(jnp.int32, mid_links.shape, 1)
    c = lax.broadcasted_iota(jnp.int32, mid_links.shape, 2)
    mid_index = (r + mid_links // 3) * (mid_cols + 2) + c + mid_links % 3
    mid_index = jnp.pad(mid_index.reshape(-1), (0, -mid_index.size % 128)).reshape(-1, 128)
    place = jnp.arange(128, dtype=jnp.int32)
    across = lax.axis_index("dx") * mid_rows - 1 + place // (mid_cols + 2)
    along = lax.axis_index("dy") * mid_cols - 1 + place % (mid_cols + 2)
    parent = (across % (4 * coarse_rows)) // 4 * coarse_cols + (along % (4 * coarse_cols)) // 4
    coarse_steps = 4
    coarse_index = coarse_links.reshape(6, coarse_steps, -1).transpose(1, 0, 2)
    coarse_index = coarse_index.reshape(coarse_steps, -1, 128)
    coarse_out, coarse_edges_new, mid_out, mid_edges_new, fine_out = run_coarse_mid(
        gathered,
        coarse_nodes.reshape(-1, feature),
        coarse_index,
        coarse_edges.reshape(6, -1, feature),
        mid_rim,
        parent[None],
        mid_index,
        mid_edges.reshape(-1, feature),
        fine_new,
        pooling[0],
        prolongation[0],
        weights,
        (mid_rows, mid_cols),
        (block_rows, block_cols, coarse_cols),
    )
    return (
        fine_out.reshape(fine_nodes.shape),
        fine_edges_new.reshape(fine_edges.shape),
        mid_out.reshape(mid_nodes.shape),
        mid_edges_new.reshape(mid_edges.shape),
        coarse_out.reshape(coarse_nodes.shape),
        coarse_edges_new.reshape(coarse_edges.shape),
    )


def solution(mesh):
    tile = P("dx", "dy", None)
    edge_tile = P(None, "dx", "dy", None)
    link_tile = P(None, "dx", "dy")
    in_specs = (tile, edge_tile, link_tile, tile, edge_tile, link_tile) + (P(),) * 18
    out_specs = (tile, edge_tile, tile, edge_tile, P(), P())
    return jax.shard_map(
        per_device, mesh=mesh, in_specs=in_specs, out_specs=out_specs, check_vma=False
    )
```

time: 356 us -> 104 us (0.29)
  blocking collectives: 178 us -> 0 us
  matrix products: 71 us -> 0 us
  Pallas kernels: 0 us -> 39.2 us
  local copies, waits for them, and re-layouts: 57.6 us -> 32.8 us
  other arithmetic: 27.2 us -> 3.33 us
  waiting for transfers between devices: 0.6 us -> 7.12 us
    all_gather x2 -> x0, blocking collectives: 178 us -> none  [all_blocks(): blocks = lax.all_gather(blocks, axes[k], axis=0, tiled=True)]
    dot_general x21 -> x0, matrix products: 71 us -> none  [the longest x3 23.7 us: level_update(): jnp.dot(flat_edges, self_matrix, preferred_element_type=jnp.float32)]
    pallas_call x0 -> x2, Pallas kernels: none -> 39.2 us  [the longest x1 23.1 us: run_fine(): pl.pallas_call(functools.partial(fine_kernel, stride), grid=(steps,), in_...]
    gather x5 -> x0, local copies, waits for them, and re-layouts: 34 us -> none  [the longest x3 30.9 us: level_update(): jnp.take(sender_terms, senders.reshape(fanout, places), axis=0)]
    unnamed x93 -> x73, local copies, waits for them, and re-layouts: 4.05 us -> 25.3 us
    ppermute x8 -> x4, starting transfers between devices: 19 us -> 9.37 us  [the longest x2 7.63 us: exchange(): after = lax.ppermute(packed(*first), axis, down)]
    all_to_all x0 -> x1, starting transfers between devices: none -> 9.59 us  [gather_coarse(): received = lax.all_to_all(slots, ('dx', 'dy'), 0, 0, tiled=True)]
    reduce_sum x11 -> x2, other arithmetic: 9.97 us -> 0.82 us  [per_device(): pooled = mid_nodes.astype(F32).reshape(block_rows, 4, block_cols, 4, feat...]
  transfers between devices with their start and end apart: 8 -> 5, of which waited for: 1 -> 2; matrix products, arithmetic and copies ran while one was open for 22% -> 7% of each run, Pallas kernels for 0% -> 23%
where the time goes in v1:
time: 104 us; the launch traced here: 103 us
  Pallas kernels  39.2 us (38%)
  local copies, waits for them, and re-layouts  32.8 us (32%)
  starting transfers between devices  19 us (18%)
  waiting for transfers between devices  7.12 us (7%)
  other arithmetic  3.33 us (3%)
  between operations  1.1 us (1%)
    unnamed x73, local copies, waits for them, and re-layouts  25.3 us
    pallas_call x1, Pallas kernels, run_fine(): pl.pallas_call(functools.partial(fine_kernel, stride), grid=(steps,), in_...  23.1 us
    pallas_call x1, Pallas kernels, run_coarse_mid(): pl.pallas_call(functools.partial(coarse_mid_kernel, steps, mid_shape, coa...  16.1 us
    all_to_all x1, starting transfers between devices, gather_coarse(): received = lax.all_to_all(slots, ('dx', 'dy'), 0, 0, tiled=True)  9.59 us
    ppermute x2, starting transfers between devices, exchange(): after = lax.ppermute(packed(*first), axis, down)  7.63 us
    ppermute x2, waiting for transfers between devices, exchange(): before = lax.ppermute(packed(*last), axis, up)  5.48 us
  transfers between devices with their start and end apart: 5, of which 2 were waited for; matrix products, arithmetic and copies ran while one was open for 7% of the time, Pallas kernels for 23%

profile of v1, /device:TPU:0, one launch (start us, length us, event | category | flops | bytes accessed | tf_op | source)
XLA Modules:
  0.0 102.5 jit_solution(12226220959716701473)
XLA Ops:
  0.6 0.0 copy-start
  0.6 0.8 slice_bitcast_fusion.5
  1.4 0.8 fusion.23
  2.3 1.7 %collective-permute-start = (bf16[52,512]{1,0:T(8,128)(2,1)S(1)}, bf16[52,512]{1,0:T(8,128)(2,1)S(1)}, u32[]{:S(2)}, u32[]{:S(2)}) collective-permute-start(bf16[52,512]{1,0:T(8,128)(2,1)S(1)} %pad_maximum_fusion.6), channel_id=1, source_target_pairs={{0,16},{16,32},{32,48},{48,64},{64,80},{80,96},{96,112},{112,0},{1... | collective-permute-start | bytes 159752 | tf_op jit(solution)/shard_map/ppermute | solution.py:360
  3.9 2.5 %collective-permute-start.1 = (bf16[52,512]{1,0:T(8,128)(2,1)S(1)}, bf16[52,512]{1,0:T(8,128)(2,1)S(1)}, u32[]{:S(2)}, u32[]{:S(2)}) collective-permute-start(bf16[52,512]{1,0:T(8,128)(2,1)S(1)} %pad_maximum_fusion.7), channel_id=1, source_target_pairs={{16,0},{32,16},{48,32},{64,48},{80,64},{96,80},{112,96},{0,112},{1... | collective-permute-start | bytes 159752 | tf_op jit(solution)/shard_map/ppermute | solution.py:361
  6.5 0.8 convert_reduce_fusion
  7.3 0.8 broadcast_in_dim.2
  8.2 9.6 %all-to-all-start = ((bf16[128,2,512]{2,1,0:T(2,128)(2,1)}), bf16[128,2,512]{2,1,0:T(2,128)(2,1)}, u32[]{:S(2)}, u32[]{:S(2)}) async-start(bf16[128,2,512]{2,1,0:T(2,128)(2,1)} %broadcast_in_dim.2), calls=%async_computation | async-start | bytes 524288 | tf_op jit(solution)/shard_map/all_to_all | solution.py:315
  17.8 0.9 fusion.12
  18.7 0.7 fusion.16
  19.4 0.8 copy.49
  20.3 0.0 copy-start.33
  20.3 0.1 pad_maximum_fusion.2
  20.4 0.1 reshape.356
  20.6 0.1 reshape.361
  20.7 0.1 copy-done.31
  20.8 0.1 copy-done.33
  20.9 5.1 %collective-permute-start.3 = (bf16[124,512]{1,0:T(8,128)(2,1)S(1)}, bf16[124,512]{1,0:T(8,128)(2,1)S(1)}, u32[]{:S(2)}, u32[]{:S(2)}) collective-permute-start(bf16[124,512]{1,0:T(8,128)(2,1)S(1)} %pad_maximum_fusion.4), channel_id=1, source_target_pairs={{1,0},{2,1},{3,2},{4,3},{5,4},{6,5},{7,6},{8,7},{9,8},{10,9},{11,1... | collective-permute-start | bytes 380936 | tf_op jit(solution)/shard_map/ppermute | solution.py:361
  26.0 0.1 collective-permute-start.2
  26.1 0.1 copy.52
  26.2 0.1 reshape.365
  26.3 0.1 reshape.347
  26.4 0.1 reshape.348.index
  26.5 0.1 copy.53
  26.6 0.1 reshape.372
  26.7 0.1 reshape.373.index
  26.8 0.1 reshape.367.mid_edges
  26.9 1.6 %collective-permute-done.3 = bf16[124,512]{1,0:T(8,128)(2,1)S(1)} collective-permute-done((bf16[124,512]{1,0:T(8,128)(2,1)S(1)}, bf16[124,512]{1,0:T(8,128)(2,1)S(1)}, u32[]{:S(2)}, u32[]{:S(2)}) %collective-permute-start.3) | collective-permute-done | bytes 127008 | tf_op jit(solution)/shard_map/ppermute | solution.py:361
  28.5 0.1 reshape.369
  28.6 5.5 %collective-permute-done.2 = bf16[124,512]{1,0:T(8,128)(2,1)S(1)} collective-permute-done((bf16[124,512]{1,0:T(8,128)(2,1)S(1)}, bf16[124,512]{1,0:T(8,128)(2,1)S(1)}, u32[]{:S(2)}, u32[]{:S(2)}) %collective-permute-start.2) | collective-permute-done | bytes 127008 | tf_op jit(solution)/shard_map/ppermute | solution.py:360
  34.1 0.7 copy-done.30
  34.7 0.1 reshape.368
  34.8 0.0 copy-start.1
  34.8 0.0 copy-start.20
  34.9 0.0 copy-start.23
  34.9 0.0 copy-start.24
  34.9 0.6 fusion.6
  35.5 0.1 pad.19.rim
  35.6 1.1 %copy-done.1 = bf16[6,32,16,512]{3,2,1,0:T(8,128)(2,1)S(1)} copy-done((bf16[6,32,16,512]{3,2,1,0:T(8,128)(2,1)S(1)}, bf16[6,32,16,512]{3,2,1,0:T(8,128)(2,1)}, u32[]{:S(2)}) %copy-start.1) | copy-done | bytes 3145752
  36.8 1.4 %copy-done.3 = bf16[1,512,1536]{2,1,0:T(8,128)(2,1)S(1)} copy-done((bf16[1,512,1536]{2,1,0:T(8,128)(2,1)S(1)}, bf16[1,512,1536]{2,1,0:T(8,128)(2,1)}, u32[]{:S(2)}) %copy-start.3) | copy-done | bytes 1572888
  38.2 1.4 %copy-done.5 = bf16[1,512,1536]{2,1,0:T(8,128)(2,1)S(1)} copy-done((bf16[1,512,1536]{2,1,0:T(8,128)(2,1)S(1)}, bf16[1,512,1536]{2,1,0:T(8,128)(2,1)}, u32[]{:S(2)}) %copy-start.5) | copy-done | bytes 1572888
  39.6 1.4 %copy-done.7 = bf16[1,512,1536]{2,1,0:T(8,128)(2,1)S(1)} copy-done((bf16[1,512,1536]{2,1,0:T(8,128)(2,1)S(1)}, bf16[1,512,1536]{2,1,0:T(8,128)(2,1)}, u32[]{:S(2)}) %copy-start.7) | copy-done | bytes 1572888
  41.0 1.4 %copy-done.9 = bf16[1,1536,512]{2,1,0:T(8,128)(2,1)S(1)} copy-done((bf16[1,1536,512]{2,1,0:T(8,128)(2,1)S(1)}, bf16[1,1536,512]{2,1,0:T(8,128)(2,1)}, u32[]{:S(2)}) %copy-start.9) | copy-done | bytes 1572888
  42.4 1.4 %copy-done.11 = bf16[1,512,1536]{2,1,0:T(8,128)(2,1)S(1)} copy-done((bf16[1,512,1536]{2,1,0:T(8,128)(2,1)S(1)}, bf16[1,512,1536]{2,1,0:T(8,128)(2,1)}, u32[]{:S(2)}) %copy-start.11) | copy-done | bytes 1572888
  43.8 1.4 %copy-done.13 = bf16[1,512,1536]{2,1,0:T(8,128)(2,1)S(1)} copy-done((bf16[1,512,1536]{2,1,0:T(8,128)(2,1)S(1)}, bf16[1,512,1536]{2,1,0:T(8,128)(2,1)}, u32[]{:S(2)}) %copy-start.13) | copy-done | bytes 1572888
  45.2 1.4 %copy-done.15 = bf16[1,1536,512]{2,1,0:T(8,128)(2,1)S(1)} copy-done((bf16[1,1536,512]{2,1,0:T(8,128)(2,1)S(1)}, bf16[1,1536,512]{2,1,0:T(8,128)(2,1)}, u32[]{:S(2)}) %copy-start.15) | copy-done | bytes 1572888
  46.6 23.1 %fine_level.1 = (bf16[512,512]{1,0:T(8,128)(2,1)S(1)}, bf16[6,512,512]{2,1,0:T(8,128)(2,1)}) custom-call(bf16[928,512]{1,0:T(8,128)(2,1)S(1)} %pad.19.rim, bf16[512,512]{1,0:T(8,128)(2,1)S(1)} %bitcast.44, s32[8,3,128]{2,1,0:T(4,128)S(1)} %reshape.373.index, bf16[6,512,512]{2,1,0:T(8,128)(2,1)S(1)} %bitcast.45, bf16[512,1536]{1,0:T(8,128)(2,1)S(1)} %bitcast.47, ...), custom_call_target="tpu_custom_call" | custom-call | flops 16106127360 | bytes 16777216 | tf_op jit(solution)/shard_map/fine_level/pallas_call | solution.py:211
  69.7 0.8 copy-done.26
  70.5 0.7 slice_bitcast_fusion
  71.3 0.7 slice_bitcast_fusion.1
  72.2 1.1 %reshape.345.pooled = bf16[256,512]{1,0:T(8,128)(2,1)S(1)} reshape(bf16[128,2,512]{2,1,0:T(2,128)(2,1)} %all-to-all-done) | data formatting | bytes 524288 | tf_op jit(solution)/shard_map/reshape | solution.py:316
  73.2 0.0 copy-start.4
  73.2 1.4 %copy-done.4 = bf16[1,512,1536]{2,1,0:T(8,128)(2,1)S(1)} copy-done((bf16[1,512,1536]{2,1,0:T(8,128)(2,1)S(1)}, bf16[1,512,1536]{2,1,0:T(8,128)(2,1)}, u32[]{:S(2)}) %copy-start.4) | copy-done | bytes 1572888
  74.6 1.4 %copy-done.6 = bf16[1,512,1536]{2,1,0:T(8,128)(2,1)S(1)} copy-done((bf16[1,512,1536]{2,1,0:T(8,128)(2,1)S(1)}, bf16[1,512,1536]{2,1,0:T(8,128)(2,1)}, u32[]{:S(2)}) %copy-start.6) | copy-done | bytes 1572888
  76.1 1.4 %copy-done.8 = bf16[1,512,1536]{2,1,0:T(8,128)(2,1)S(1)} copy-done((bf16[1,512,1536]{2,1,0:T(8,128)(2,1)S(1)}, bf16[1,512,1536]{2,1,0:T(8,128)(2,1)}, u32[]{:S(2)}) %copy-start.8) | copy-done | bytes 1572888
  77.5 1.4 %copy-done.10 = bf16[1,1536,512]{2,1,0:T(8,128)(2,1)S(1)} copy-done((bf16[1,1536,512]{2,1,0:T(8,128)(2,1)S(1)}, bf16[1,1536,512]{2,1,0:T(8,128)(2,1)}, u32[]{:S(2)}) %copy-start.10) | copy-done | bytes 1572888
  78.9 1.4 %copy-done.12 = bf16[1,512,1536]{2,1,0:T(8,128)(2,1)S(1)} copy-done((bf16[1,512,1536]{2,1,0:T(8,128)(2,1)S(1)}, bf16[1,512,1536]{2,1,0:T(8,128)(2,1)}, u32[]{:S(2)}) %copy-start.12) | copy-done | bytes 1572888
  80.3 1.4 %copy-done.14 = bf16[1,512,1536]{2,1,0:T(8,128)(2,1)S(1)} copy-done((bf16[1,512,1536]{2,1,0:T(8,128)(2,1)S(1)}, bf16[1,512,1536]{2,1,0:T(8,128)(2,1)}, u32[]{:S(2)}) %copy-start.14) | copy-done | bytes 1572888
  81.7 1.4 %copy-done.16 = bf16[1,1536,512]{2,1,0:T(8,128)(2,1)S(1)} copy-done((bf16[1,1536,512]{2,1,0:T(8,128)(2,1)S(1)}, bf16[1,1536,512]{2,1,0:T(8,128)(2,1)}, u32[]{:S(2)}) %copy-start.16) | copy-done | bytes 1572888
  83.1 0.9 copy-done.19
  84.0 1.0 %copy-done.27 = bf16[512,512]{1,0:T(8,128)(2,1)S(1)} copy-done((bf16[512,512]{1,0:T(8,128)(2,1)S(1)}, bf16[512,512]{1,0:T(8,128)(2,1)}, u32[]{:S(2)}) %copy-start.27) | copy-done | bytes 524312
  85.1 16.1 %coarse_mid_levels.1 = (bf16[256,512]{1,0:T(8,128)(2,1)}, bf16[6,256,512]{2,1,0:T(8,128)(2,1)}, bf16[32,512]{1,0:T(8,128)(2,1)S(1)}, bf16[192,512]{1,0:T(8,128)(2,1)S(1)}, bf16[512,512]{1,0:T(8,128)(2,1)}) custom-call(bf16[256,512]{1,0:T(8,128)(2,1)S(1)} %reshape.345.pooled, bf16[256,512]{1,0:T(8,128)(2,1)S(1)} %bitcast.63, ...), custom_call_target="tpu_custom_call" | custom-call | flops 8053063680 | bytes 8388608 | tf_op jit(solution)/shard_map/coarse_mid_levels/pallas_call | solution.py:263
  101.2 0.6 reshape.377
  101.8 0.7 reshape.378
  (73 shorter events, 0.4 us)
Async XLA Ops:
  0.6 19.7 %copy-start = (bf16[32,16,512]{2,1,0:T(8,128)(2,1)S(1)}, bf16[32,16,512]{2,1,0:T(8,128)(2,1)}, u32[]{:S(2)}) copy-start(bf16[32,16,512]{2,1,0:T(8,128)(2,1)} %param.24) | copy-start | bytes 1572868
  2.2 24.1 %copy-start.35 = (s32[6,16,16]{2,1,0:T(8,128)S(1)}, s32[6,16,16]{2,1,0:T(8,128)}, u32[]{:S(2)}) copy-start(s32[6,16,16]{2,1,0:T(8,128)} %param.32) | copy-start | bytes 18436
  2.3 17.9 %collective-permute-start = (bf16[52,512]{1,0:T(8,128)(2,1)S(1)}, bf16[52,512]{1,0:T(8,128)(2,1)S(1)}, u32[]{:S(2)}, u32[]{:S(2)}) collective-permute-start(bf16[52,512]{1,0:T(8,128)(2,1)S(1)} %pad_maximum_fusion.6), channel_id=1, source_target_pairs={{0,16},{16,32},{32,48},{48,64},{64,80},{80,96},{96,112},{112,0},{1... | collective-permute-start | bytes 159752 | tf_op jit(solution)/shard_map/ppermute | solution.py:360
  3.9 16.3 %collective-permute-start.1 = (bf16[52,512]{1,0:T(8,128)(2,1)S(1)}, bf16[52,512]{1,0:T(8,128)(2,1)S(1)}, u32[]{:S(2)}, u32[]{:S(2)}) collective-permute-start(bf16[52,512]{1,0:T(8,128)(2,1)S(1)} %pad_maximum_fusion.7), channel_id=1, source_target_pairs={{16,0},{32,16},{48,32},{64,48},{80,64},{96,80},{112,96},{0,112},{1... | collective-permute-start | bytes 159752 | tf_op jit(solution)/shard_map/ppermute | solution.py:361
  8.2 18.6 %copy-start.28 = (bf16[6,8,4,512]{3,2,1,0:T(4,128)(2,1)S(1)}, bf16[6,8,4,512]{3,2,1,0:T(4,128)(2,1)}, u32[]{:S(2)}) copy-start(bf16[6,8,4,512]{3,2,1,0:T(4,128)(2,1)} %param.28) | copy-start | bytes 589828
  8.2 64.0 %all-to-all-start = ((bf16[128,2,512]{2,1,0:T(2,128)(2,1)}), bf16[128,2,512]{2,1,0:T(2,128)(2,1)}, u32[]{:S(2)}, u32[]{:S(2)}) async-start(bf16[128,2,512]{2,1,0:T(2,128)(2,1)} %broadcast_in_dim.2), calls=%async_computation | async-start | bytes 524288 | tf_op jit(solution)/shard_map/all_to_all | solution.py:315
  20.2 0.6 copy-start.31
  20.3 0.6 copy-start.33
  20.9 7.6 %collective-permute-start.3 = (bf16[124,512]{1,0:T(8,128)(2,1)S(1)}, bf16[124,512]{1,0:T(8,128)(2,1)S(1)}, u32[]{:S(2)}, u32[]{:S(2)}) collective-permute-start(bf16[124,512]{1,0:T(8,128)(2,1)S(1)} %pad_maximum_fusion.4), channel_id=1, source_target_pairs={{1,0},{2,1},{3,2},{4,3},{5,4},{6,5},{7,6},{8,7},{9,8},{10,9},{11,1... | collective-permute-start | bytes 380936 | tf_op jit(solution)/shard_map/ppermute | solution.py:361
  26.0 8.1 %collective-permute-start.2 = (bf16[124,512]{1,0:T(8,128)(2,1)S(1)}, bf16[124,512]{1,0:T(8,128)(2,1)S(1)}, u32[]{:S(2)}, u32[]{:S(2)}) collective-permute-start(bf16[124,512]{1,0:T(8,128)(2,1)S(1)} %pad_maximum_fusion.3), channel_id=1, source_target_pairs={{0,1},{1,2},{2,3},{3,4},{4,5},{5,6},{6,7},{7,8},{8,9},{9,10},{10,1... | collective-permute-start | bytes 380936 | tf_op jit(solution)/shard_map/ppermute | solution.py:360
  28.5 6.2 %copy-start.29 = (bf16[124,512]{1,0:T(8,128)(2,1)}, bf16[124,512]{1,0:T(8,128)(2,1)S(1)}, u32[]{:S(2)}) copy-start(bf16[124,512]{1,0:T(8,128)(2,1)S(1)} %collective-permute-done.3) | copy-start | bytes 380932
  34.1 0.7 copy-start.30
  34.8 1.9 %copy-start.1 = (bf16[6,32,16,512]{3,2,1,0:T(8,128)(2,1)S(1)}, bf16[6,32,16,512]{3,2,1,0:T(8,128)(2,1)}, u32[]{:S(2)}) copy-start(bf16[6,32,16,512]{3,2,1,0:T(8,128)(2,1)} %param.25) | copy-start | bytes 9437188
  34.8 1.9 %copy-start.20 = (f32[1,1536]{1,0:T(1,128)S(1)}, f32[1,1536]{1,0:T(1,128)}, u32[]{:S(2)}) copy-start(f32[1,1536]{1,0:T(1,128)} %refs_3_.3) | copy-start | bytes 18436
  34.8 1.9 %copy-start.21 = (f32[1,1536]{1,0:T(1,128)S(1)}, f32[1,1536]{1,0:T(1,128)}, u32[]{:S(2)}) copy-start(f32[1,1536]{1,0:T(1,128)} %refs_9_.3) | copy-start | bytes 18436
  34.9 1.9 %copy-start.22 = (f32[1,512]{1,0:T(1,128)S(1)}, f32[1,512]{1,0:T(1,128)}, u32[]{:S(2)}) copy-start(f32[1,512]{1,0:T(1,128)} %refs_5_.3) | copy-start | bytes 6148
  34.9 1.9 %copy-start.23 = (f32[1,512]{1,0:T(1,128)S(1)}, f32[1,512]{1,0:T(1,128)}, u32[]{:S(2)}) copy-start(f32[1,512]{1,0:T(1,128)} %refs_6_.3) | copy-start | bytes 6148
  34.9 1.8 %copy-start.24 = (f32[1,512]{1,0:T(1,128)S(1)}, f32[1,512]{1,0:T(1,128)}, u32[]{:S(2)}) copy-start(f32[1,512]{1,0:T(1,128)} %refs_11_.3) | copy-start | bytes 6148
  34.9 1.8 %copy-start.25 = (f32[1,512]{1,0:T(1,128)S(1)}, f32[1,512]{1,0:T(1,128)}, u32[]{:S(2)}) copy-start(f32[1,512]{1,0:T(1,128)} %refs_12_.3) | copy-start | bytes 6148
  36.7 1.4 %copy-start.3 = (bf16[1,512,1536]{2,1,0:T(8,128)(2,1)S(1)}, bf16[1,512,1536]{2,1,0:T(8,128)(2,1)}, u32[]{:S(2)}) copy-start(bf16[1,512,1536]{2,1,0:T(8,128)(2,1)} %param.33) | copy-start | bytes 4718596
  38.2 1.4 %copy-start.5 = (bf16[1,512,1536]{2,1,0:T(8,128)(2,1)S(1)}, bf16[1,512,1536]{2,1,0:T(8,128)(2,1)}, u32[]{:S(2)}) copy-start(bf16[1,512,1536]{2,1,0:T(8,128)(2,1)} %param.34) | copy-start | bytes 4718596
  39.6 1.4 %copy-start.7 = (bf16[1,512,1536]{2,1,0:T(8,128)(2,1)S(1)}, bf16[1,512,1536]{2,1,0:T(8,128)(2,1)}, u32[]{:S(2)}) copy-start(bf16[1,512,1536]{2,1,0:T(8,128)(2,1)} %param.35) | copy-start | bytes 4718596
  41.0 1.4 %copy-start.9 = (bf16[1,1536,512]{2,1,0:T(8,128)(2,1)S(1)}, bf16[1,1536,512]{2,1,0:T(8,128)(2,1)}, u32[]{:S(2)}) copy-start(bf16[1,1536,512]{2,1,0:T(8,128)(2,1)} %param.37) | copy-start | bytes 4718596
  42.4 1.4 %copy-start.11 = (bf16[1,512,1536]{2,1,0:T(8,128)(2,1)S(1)}, bf16[1,512,1536]{2,1,0:T(8,128)(2,1)}, u32[]{:S(2)}) copy-start(bf16[1,512,1536]{2,1,0:T(8,128)(2,1)} %param.40) | copy-start | bytes 4718596
  43.8 1.4 %copy-start.13 = (bf16[1,512,1536]{2,1,0:T(8,128)(2,1)S(1)}, bf16[1,512,1536]{2,1,0:T(8,128)(2,1)}, u32[]{:S(2)}) copy-start(bf16[1,512,1536]{2,1,0:T(8,128)(2,1)} %param.41) | copy-start | bytes 4718596
  45.2 1.4 %copy-start.15 = (bf16[1,1536,512]{2,1,0:T(8,128)(2,1)S(1)}, bf16[1,1536,512]{2,1,0:T(8,128)(2,1)}, u32[]{:S(2)}) copy-start(bf16[1,1536,512]{2,1,0:T(8,128)(2,1)} %param.43) | copy-start | bytes 4718596
  46.6 25.4 %copy-start.32 = (bf16[1,4,512]{2,0,1:T(2,128)(2,1)S(1)}, bf16[1,4,512]{2,0,1:T(2,128)(2,1)}, u32[]{:S(2)}) copy-start(bf16[1,4,512]{2,0,1:T(2,128)(2,1)} %copy-done.31) | copy-start | bytes 12292
  46.6 25.4 %copy-start.34 = (bf16[1,4,512]{2,0,1:T(2,128)(2,1)S(1)}, bf16[1,4,512]{2,0,1:T(2,128)(2,1)}, u32[]{:S(2)}) copy-start(bf16[1,4,512]{2,0,1:T(2,128)(2,1)} %copy-done.33) | copy-start | bytes 12292
  46.6 26.6 %copy-start.2 = (bf16[6,16,16,512]{3,2,1,0:T(8,128)(2,1)S(1)}, bf16[6,16,16,512]{3,2,1,0:T(8,128)(2,1)}, u32[]{:S(2)}) copy-start(bf16[6,16,16,512]{3,2,1,0:T(8,128)(2,1)} %param.31) | copy-start | bytes 4718596
  46.6 26.6 %copy-start.17 = (bf16[1,512,512]{2,1,0:T(8,128)(2,1)S(1)}, bf16[1,512,512]{2,1,0:T(8,128)(2,1)}, u32[]{:S(2)}) copy-start(bf16[1,512,512]{2,1,0:T(8,128)(2,1)} %param.47) | copy-start | bytes 1572868
  46.6 26.6 %copy-start.18 = (bf16[1,512,512]{2,1,0:T(8,128)(2,1)S(1)}, bf16[1,512,512]{2,1,0:T(8,128)(2,1)}, u32[]{:S(2)}) copy-start(bf16[1,512,512]{2,1,0:T(8,128)(2,1)} %param.46) | copy-start | bytes 1572868
  69.7 0.8 copy-start.26
  73.2 1.4 %copy-start.4 = (bf16[1,512,1536]{2,1,0:T(8,128)(2,1)S(1)}, bf16[1,512,1536]{2,1,0:T(8,128)(2,1)}, u32[]{:S(2)}) copy-start(bf16[1,512,1536]{2,1,0:T(8,128)(2,1)} %param.33) | copy-start | bytes 4718596
  74.6 1.4 %copy-start.6 = (bf16[1,512,1536]{2,1,0:T(8,128)(2,1)S(1)}, bf16[1,512,1536]{2,1,0:T(8,128)(2,1)}, u32[]{:S(2)}) copy-start(bf16[1,512,1536]{2,1,0:T(8,128)(2,1)} %param.34) | copy-start | bytes 4718596
  76.1 1.4 %copy-start.8 = (bf16[1,512,1536]{2,1,0:T(8,128)(2,1)S(1)}, bf16[1,512,1536]{2,1,0:T(8,128)(2,1)}, u32[]{:S(2)}) copy-start(bf16[1,512,1536]{2,1,0:T(8,128)(2,1)} %param.35) | copy-start | bytes 4718596
  77.5 1.4 %copy-start.10 = (bf16[1,1536,512]{2,1,0:T(8,128)(2,1)S(1)}, bf16[1,1536,512]{2,1,0:T(8,128)(2,1)}, u32[]{:S(2)}) copy-start(bf16[1,1536,512]{2,1,0:T(8,128)(2,1)} %param.37) | copy-start | bytes 4718596
  78.9 1.4 %copy-start.12 = (bf16[1,512,1536]{2,1,0:T(8,128)(2,1)S(1)}, bf16[1,512,1536]{2,1,0:T(8,128)(2,1)}, u32[]{:S(2)}) copy-start(bf16[1,512,1536]{2,1,0:T(8,128)(2,1)} %param.40) | copy-start | bytes 4718596
  80.3 1.4 %copy-start.14 = (bf16[1,512,1536]{2,1,0:T(8,128)(2,1)S(1)}, bf16[1,512,1536]{2,1,0:T(8,128)(2,1)}, u32[]{:S(2)}) copy-start(bf16[1,512,1536]{2,1,0:T(8,128)(2,1)} %param.41) | copy-start | bytes 4718596
  81.7 1.4 %copy-start.16 = (bf16[1,1536,512]{2,1,0:T(8,128)(2,1)S(1)}, bf16[1,1536,512]{2,1,0:T(8,128)(2,1)}, u32[]{:S(2)}) copy-start(bf16[1,1536,512]{2,1,0:T(8,128)(2,1)} %param.43) | copy-start | bytes 4718596
  83.1 0.9 copy-start.19
  84.0 1.0 %copy-start.27 = (bf16[512,512]{1,0:T(8,128)(2,1)S(1)}, bf16[512,512]{1,0:T(8,128)(2,1)}, u32[]{:S(2)}) copy-start(bf16[512,512]{1,0:T(8,128)(2,1)} %copy-done.26) | copy-start | bytes 1572868
